TPU v7x, 32 devices: a whole 2x2x4 slice. The times are simulated.
32 devices in a mesh: groups: 2 (over y), vocab: 4 (over z), edit: 2 (over x), tok: 2 (over core).
Axes of the slice: x: 2, y: 2, z: 4, core: 2. Of those that a mesh axis runs over, the one named last changes fastest.
Arguments:
- token_ids: int32 [256], P(('groups', 'tok')), parts along dimension 0, may hold values from 0 to 4095
- valid_mask: int32 [256], P(('groups', 'tok')), parts along dimension 0, may hold values 0 or 1
- key_index: int32 [4], P('groups'), parts along dimension 0, may hold values from 0 to 3
- hidden_act: bfloat16 [256, 14336], P(('groups', 'tok'), 'vocab'), parts along dimension 0, may hold values from -6 to 6
- key_table: bfloat16 [4, 14336], P(None, 'vocab'), may hold values from -0.046875 to 0.046875
- base_out: bfloat16 [256, 4096], P(('groups', 'tok'), 'vocab'), parts along dimension 0, may hold values from -50 to 50
- value_vecs: bfloat16 [4, 4096], P(('groups', 'edit'), 'vocab'), parts along dimension 0, may hold values from -6 to 6
- norm_gain: float32 [4096], replicated, may hold values from 0.5 to 1.5
- head: bfloat16 [4096, 4096], P(('vocab', 'edit')), may hold values from -46 to 46
Outputs:
- grad_value: float32 [4, 4096], P(('groups', 'edit'), 'vocab'), parts along dimension 0
- token_kl: float32 [4, 128], P(('groups', 'edit'), 'tok'), parts along dimension 0
- target_logprob: float32 [4, 128], P(('groups', 'edit'), 'tok'), parts along dimension 0
There are 2 independent parts, one for each index of `groups`. A program takes and returns all parts, laid end to end along the dimension named above; an argument that names none is the same for every part. Nothing has to cross between parts.
All inputs are finite; a program needn't handle non-finite values. No bound on the sum of `valid_mask` on one device may be relied on, other than what follows from the above.
Results may differ from a plain program's by a relative error of at most 0.0061.
Values may be sent and summed in bfloat16 or wider, within the bound.
A program may use at most 64 MiB of HBM per device.

v0:
```python
import jax
import jax.numpy as jnp
from jax import lax
from jax.sharding import PartitionSpec as P

NORM_EPS = 1e-05


def rms_scale(hidden_rows):
    return lax.rsqrt(jnp.mean(hidden_rows * hidden_rows, axis=-1, keepdims=True) + NORM_EPS)


def per_device(
    token_ids, valid_mask, key_index, hidden_act, key_table, base_out, value_vecs, norm_gain, head
):
    vocab_rows = head.shape[0]
    edit_rows = value_vecs.shape[0]
    piece_width = value_vecs.shape[1]
    key_slots = jnp.arange(key_table.shape[0], dtype=jnp.int32)
    select = (key_index[:, None] == key_slots[None, :]).astype(jnp.bfloat16)
    edit_keys = jnp.dot(select, key_table, preferred_element_type=jnp.float32).astype(jnp.bfloat16)
    coeff_part = lax.dot_general(
        edit_keys, hidden_act, (((1,), (1,)), ((), ())), preferred_element_type=jnp.float32
    )
    coeff = lax.psum(coeff_part, "vocab")
    base_rows, local_values = (
        lax.all_gather(base_out, "vocab", axis=1, tiled=True),
        lax.all_gather(value_vecs, "vocab", axis=1, tiled=True),
    )
    values = lax.all_gather(local_values, "edit", axis=0, tiled=True)
    base32 = base_rows.astype(jnp.float32)
    base_norm = (norm_gain * base32 * rms_scale(base32)).astype(jnp.bfloat16)
    base_logits = lax.dot_general(
        base_norm, head, (((1,), (1,)), ((), ())), preferred_element_type=jnp.float32
    )
    edited = base32[None, :, :] + coeff[:, :, None] * values.astype(jnp.float32)[:, None, :]
    row_scale = rms_scale(edited)
    normed = (norm_gain * edited * row_scale).astype(jnp.bfloat16)
    logits = jnp.einsum("etd,vd->etv", normed, head, preferred_element_type=jnp.float32)
    vocab_start = lax.axis_index(("vocab", "edit")) * vocab_rows
    vocab_ids = vocab_start + jnp.arange(vocab_rows, dtype=jnp.int32)
    onehot = (token_ids[:, None] == vocab_ids[None, :]).astype(jnp.float32)
    peak_base = jnp.max(base_logits, axis=-1)
    peak_edit = jnp.max(logits, axis=-1)
    peak_base, peak_edit = lax.pmax((peak_base, peak_edit), ("vocab", "edit"))
    base_exp = jnp.exp(base_logits - peak_base[:, None])
    base_total = jnp.sum(base_exp, axis=-1)
    edit_total = jnp.sum(jnp.exp(logits - peak_edit[:, :, None]), axis=-1)
    cross_sum = jnp.sum(base_exp[None, :, :] * (base_logits[None, :, :] - logits), axis=-1)
    target = jnp.sum(onehot[None, :, :] * logits, axis=-1)
    base_total, edit_total, cross_sum, target = lax.psum(
        (base_total, edit_total, cross_sum, target), ("vocab", "edit")
    )
    base_lse = peak_base + jnp.log(base_total)
    edit_lse = peak_edit + jnp.log(edit_total)
    valid = valid_mask.astype(jnp.float32)
    token_kl = valid[None, :] * (cross_sum / base_total[None, :] - base_lse[None, :] + edit_lse)
    target_logprob = target - edit_lse
    base_prob = jnp.exp(base_logits - base_lse[:, None])
    edit_prob = jnp.exp(logits - edit_lse[:, :, None])
    logit_grad = (valid[None, :, None] * (edit_prob - base_prob[None, :, :])).astype(jnp.bfloat16)
    back_rows = jnp.einsum("etv,vd->etd", logit_grad, head, preferred_element_type=jnp.float32)
    grad_y = norm_gain * back_rows
    grad_o = row_scale * grad_y - edited * row_scale**3 * jnp.mean(
        grad_y * edited, axis=-1, keepdims=True
    )
    grad_part = jnp.sum(coeff[:, :, None] * grad_o, axis=1)
    edit_start = lax.axis_index("edit") * edit_rows
    grad_total = lax.psum(grad_part, ("vocab", "edit", "tok"))
    grad_mine = lax.dynamic_slice_in_dim(grad_total, edit_start, edit_rows, 0)
    grad_piece = lax.dynamic_slice_in_dim(
        grad_mine, lax.axis_index("vocab") * piece_width, piece_width, 1
    )
    kl_mine = lax.dynamic_slice_in_dim(token_kl, edit_start, edit_rows, 0)
    target_mine = lax.dynamic_slice_in_dim(target_logprob, edit_start, edit_rows, 0)
    return (grad_piece, kl_mine, target_mine)


def solution(mesh):
    placed = (
        P(("groups", "tok")),
        P(("groups", "tok")),
        P("groups"),
        P(("groups", "tok"), "vocab"),
        P(None, "vocab"),
        P(("groups", "tok"), "vocab"),
        P(("groups", "edit"), "vocab"),
        P(),
        P(("vocab", "edit"), None),
    )
    return jax.shard_map(
        per_device,
        mesh=mesh,
        in_specs=placed,
        out_specs=(
            P(("groups", "edit"), "vocab"),
            P(("groups", "edit"), "tok"),
            P(("groups", "edit"), "tok"),
        ),
        check_vma=False,
    )
```

profile of v0, /device:TPU:0, one launch (start us, length us, event | category | flops | bytes accessed | tf_op | source)
XLA Modules:
  0.0 156.0 jit_solution(18408327459742363050)
XLA Ops:
  0.7 0.7 convert_element_type.32
  1.4 0.3 copy-done
  1.7 1.1 fusion.3
  2.8 13.4 %psum.42 = f32[2,64]{1,0:T(2,128)S(1)} all-reduce(f32[2,64]{1,0:T(2,128)S(1)} %fusion.3), channel_id=1, replica_groups=mesh['groups'=2,'vocab'=4,'edit'=2,'tok'=2] {'vocab'}, use_global_device_ids=true, to_apply=%region_0.0 | all-reduce | flops 128 | bytes 1024 | tf_op jit(solution)/shard_map/psum | solution.py:25
  16.3 13.3 %all_gather.10 = bf16[1,4096]{1,0:T(2,128)(2,1)S(1)} all-gather(bf16[1,1024]{1,0:T(2,128)(2,1)} %param.15), channel_id=1, replica_groups=mesh['groups'=2,'vocab'=4,'edit'=2,'tok'=2] {'vocab'}, dimensions={1}, use_global_device_ids=true | all-gather | bytes 10240 | tf_op jit(solution)/shard_map/all_gather | solution.py:28
  29.5 4.4 %all-gather = bf16[2,1,4096]{2,1,0:T(2,128)(2,1)S(1)} all-gather(bf16[1,1,4096]{2,1,0:T(2,128)(2,1)S(1)} %bitcast.20), channel_id=1, replica_groups=mesh['groups'=2,'vocab'=4,'edit'=2,'tok'=2] {'edit'}, dimensions={0}, use_global_device_ids=true | all-gather | bytes 24576 | tf_op jit(solution)/shard_map/all_gather | solution.py:30
  34.0 0.7 compare_convert_fusion
  34.7 15.0 %all_gather.9 = bf16[64,4096]{1,0:T(8,128)(2,1)S(1)} all-gather(bf16[64,1024]{1,0:T(8,128)(2,1)} %param.14), channel_id=1, replica_groups=mesh['groups'=2,'vocab'=4,'edit'=2,'tok'=2] {'vocab'}, dimensions={1}, use_global_device_ids=true | all-gather | bytes 655360 | tf_op jit(solution)/shard_map/all_gather | solution.py:27
  49.7 0.2 multiply_reduce_fusion.3
  49.9 3.9 %fusion.24 = (f32[64]{0:T(128)S(1)}, f32[64,512]{1,0:T(8,128)S(1)}) fusion(bf16[512,4096]{1,0:T(8,128)(2,1)} %param.17, f32[64]{0:T(128)S(1)} %add_rsqrt_fusion.1, f32[4096]{0:T(1024)} %param.16, bf16[64,4096]{1,0:T(8,128)(2,1)S(1)} %all_gather.9), kind=kOutput, calls=%fused_computation.48 | convolution fusion | flops 269516736 | bytes 4866560 | tf_op jit(solution)/shard_map/dot_general | solution.py:33
  53.8 0.1 convert_element_type.30
  53.9 0.4 multiply_reduce_fusion.2
  54.3 0.2 copy-done.2
  54.5 1.6 %fusion.25 = (f32[2,64]{1,0:T(2,128)S(1)}, f32[2,64,512]{2,1,0:T(8,128)S(1)}) fusion(bf16[512,4096]{1,0:T(8,128)(2,1)S(1)} %copy-done.1, f32[4096]{0:T(1024)S(1)} %copy-done.2, f32[2,64]{1,0:T(2,128)S(1)} %get-tuple-element.17, f32[2,4096]{1,0:T(2,128)S(1)} %bitcast.17, f32[64,4096]{1,0:T(8,128)S(1)} %convert_element_type.30, f32[2,64]{1,0:T(2,128)S(1)} %psum.42), kind=kOutput, calls=%fused_computation.49 | convolution fusion | flops 539557760 | bytes 5555712 | tf_op jit(solution)/shard_map/etd,vd->etv/dot_general | solution.py:39
  56.1 18.6 %all-reduce.1 = (f32[64]{0:T(128)S(1)}, f32[2,64]{1,0:T(2,128)S(1)}) all-reduce(f32[64]{0:T(128)S(1)} %get-tuple-element.18, f32[2,64]{1,0:T(2,128)S(1)} %get-tuple-element.20), channel_id=1, replica_groups=mesh['groups'=2,'vocab'=4,'edit'=2,'tok'=2] {'vocab','edit'}, use_global_device_ids=true, to_apply=%region_8.0 | all-reduce | flops 192 | bytes 1536 | tf_op jit(solution)/shard_map/pmax | solution.py:45
  74.7 0.2 fusion.23
  74.9 0.2 multiply_reduce_fusion.4
  75.1 17.7 %all-reduce = (f32[64]{0:T(128)S(1)}, f32[2,64]{1,0:T(2,128)S(1)}, f32[2,64]{1,0:T(2,128)S(1)}, f32[2,64]{1,0:T(2,128)S(1)}) all-reduce(f32[64]{0:T(128)S(1)} %get-tuple-element.14, f32[2,64]{1,0:T(2,128)S(1)} %get-tuple-element.5, ...), channel_id=1, replica_groups=mesh['groups'=2,'vocab'=4,'edit'=2,'tok'=2] {'vocab','edit'}, use_global_device_ids=true, to_apply=%region_10.0 | all-reduce | flops 448 | bytes 3584 | tf_op jit(solution)/shard_map/psum | solution.py:51
  92.8 0.1 subtract_exponential_fusion
  92.9 0.5 constant_dynamic-slice_fusion
  93.4 3.4 %multiply_reduce_fusion.1 = (f32[2,64]{1,0:T(2,128)S(1)}, f32[2,64,4096]{2,1,0:T(8,128)S(1)}) fusion(f32[2,4096]{1,0:T(2,128)S(1)} %bitcast.18, f32[64,4096]{1,0:T(8,128)S(1)} %convert_element_type.30, f32[2,64]{1,0:T(2,128)S(1)} %psum.42, bf16[512,4096]{1,0:T(8,128)(2,1)} %param.17, f32[2,64,512]{2,1,0:T(8,128)S(1)} %get-tuple-element.21, ...), kind=kOutput, calls=%fused_computation.6 | convolution fusion | flops 539754368 | bytes 7784192 | tf_op jit(solution)/shard_map/etv,vd->etd/dot_general | solution.py:62
  96.9 0.8 multiply_reduce_fusion
  97.7 57.6 %psum.45 = f32[2,4096]{1,0:T(2,128)S(1)} all-reduce(f32[2,4096]{1,0:T(2,128)S(1)} %multiply_reduce_fusion), channel_id=1, replica_groups=mesh['groups'=2,'vocab'=4,'edit'=2,'tok'=2] {'vocab','edit','tok'}, use_global_device_ids=true, to_apply=%region_13.0 | all-reduce | flops 8192 | bytes 65536 | tf_op jit(solution)/shard_map/psum | solution.py:69
  155.3 0.7 dynamic_slice.10
  (12 shorter events, 0.1 us)
Async XLA Ops:
  0.6 1.0 copy-start
  49.9 4.4 %copy-start.1 = (bf16[512,4096]{1,0:T(8,128)(2,1)S(1)}, bf16[512,4096]{1,0:T(8,128)(2,1)}, u32[]{:S(2)}) copy-start(bf16[512,4096]{1,0:T(8,128)(2,1)} %param.17) | copy-start | bytes 12582916
  53.8 0.7 copy-start.2
where the time goes:
time: 156 us
  blocking collectives  140 us (90%)
  matrix products  10 us (6%)
  other arithmetic  3.51 us (2%)
  local copies, waits for them, and re-layouts  1.73 us (1%)
    psum x1, blocking collectives, per_device(): grad_total = lax.psum(grad_part, ('vocab', 'edit', 'tok'))  57.6 us
    pmax x1, blocking collectives, per_device(): peak_base, peak_edit = lax.pmax((peak_base, peak_edit), ('vocab', 'edit'))  18.6 us
    psum x1, blocking collectives, per_device(): lax.psum((base_total, edit_total, cross_sum, target), ('vocab', 'edit'))  17.7 us
    all_gather x1, blocking collectives, per_device(): lax.all_gather(base_out, 'vocab', axis=1, tiled=True)  15 us
    psum x1, blocking collectives, per_device(): coeff = lax.psum(coeff_part, 'vocab')  13.4 us
    all_gather x1, blocking collectives, per_device(): lax.all_gather(value_vecs, 'vocab', axis=1, tiled=True)  13.3 us
    all_gather x1, blocking collectives, per_device(): values = lax.all_gather(local_values, 'edit', axis=0, tiled=True)  4.4 us
    dot_general x1, matrix products, per_device(): lax.dot_general(base_norm, head, (((1,), (1,)), ((), ())), preferred_elem...  3.87 us

commit v1 on v0

--- a/solution.py
+++ b/solution.py
@@ -49,7 +49,7 @@
     cross_sum = jnp.sum(base_exp[None, :, :] * (base_logits[None, :, :] - logits), axis=-1)
     target = jnp.sum(onehot[None, :, :] * logits, axis=-1)
     base_total, edit_total, cross_sum, target = lax.psum(
-        (base_total, edit_total, cross_sum, target), ("vocab", "edit")
+        lax.psum((base_total, edit_total, cross_sum, target), "edit"), "vocab"
     )
     base_lse = peak_base + jnp.log(base_total)
     edit_lse = peak_edit + jnp.log(edit_total)

time: 156 us -> 152 us (0.974)
  blocking collectives: 140 us -> 136 us
    psum x1 -> x2, blocking collectives: 17.7 us -> 13.3 us  [the longest x1 8.34 us: per_device(): lax.psum(lax.psum((base_total, edit_total, cross_sum, target), 'edit'), '...]
where the time goes in v1:
time: 152 us
  blocking collectives  136 us (89%)
  matrix products  10 us (7%)
  other arithmetic  3.51 us (2%)
  local copies, waits for them, and re-layouts  1.73 us (1%)
    psum x1, blocking collectives, per_device(): grad_total = lax.psum(grad_part, ('vocab', 'edit', 'tok'))  57.6 us
    pmax x1, blocking collectives, per_device(): peak_base, peak_edit = lax.pmax((peak_base, peak_edit), ('vocab', 'edit'))  18.6 us
    all_gather x1, blocking collectives, per_device(): lax.all_gather(base_out, 'vocab', axis=1, tiled=True)  15 us
    psum x1, blocking collectives, per_device(): coeff = lax.psum(coeff_part, 'vocab')  13.4 us
    all_gather x1, blocking collectives, per_device(): lax.all_gather(value_vecs, 'vocab', axis=1, tiled=True)  13.3 us
    psum x1, blocking collectives, per_device(): lax.psum(lax.psum((base_total, edit_total, cross_sum, target), 'edit'), '...  8.34 us
    psum x1, blocking collectives, per_device(): lax.psum((base_total, edit_total, cross_sum, target), 'edit')  4.94 us
    all_gather x1, blocking collectives, per_device(): values = lax.all_gather(local_values, 'edit', axis=0, tiled=True)  4.4 us

profile of v1, /device:TPU:0, one launch (start us, length us, event | category | flops | bytes accessed | tf_op | source)
XLA Modules:
  0.0 151.6 jit_solution(2416265030503797968)
XLA Ops:
  0.7 0.7 convert_element_type.32
  1.4 0.3 copy-done
  1.7 1.1 fusion.3
  2.8 13.4 %psum.70 = f32[2,64]{1,0:T(2,128)S(1)} all-reduce(f32[2,64]{1,0:T(2,128)S(1)} %fusion.3), channel_id=1, replica_groups=mesh['groups'=2,'vocab'=4,'edit'=2,'tok'=2] {'vocab'}, use_global_device_ids=true, to_apply=%region_0.0 | all-reduce | flops 128 | bytes 1024 | tf_op jit(solution)/shard_map/psum | solution.py:25
  16.3 13.3 %all_gather.10 = bf16[1,4096]{1,0:T(2,128)(2,1)S(1)} all-gather(bf16[1,1024]{1,0:T(2,128)(2,1)} %param.15), channel_id=1, replica_groups=mesh['groups'=2,'vocab'=4,'edit'=2,'tok'=2] {'vocab'}, dimensions={1}, use_global_device_ids=true | all-gather | bytes 10240 | tf_op jit(solution)/shard_map/all_gather | solution.py:28
  29.5 4.4 %all-gather = bf16[2,1,4096]{2,1,0:T(2,128)(2,1)S(1)} all-gather(bf16[1,1,4096]{2,1,0:T(2,128)(2,1)S(1)} %bitcast.20), channel_id=1, replica_groups=mesh['groups'=2,'vocab'=4,'edit'=2,'tok'=2] {'edit'}, dimensions={0}, use_global_device_ids=true | all-gather | bytes 24576 | tf_op jit(solution)/shard_map/all_gather | solution.py:30
  34.0 0.7 compare_convert_fusion
  34.7 15.0 %all_gather.9 = bf16[64,4096]{1,0:T(8,128)(2,1)S(1)} all-gather(bf16[64,1024]{1,0:T(8,128)(2,1)} %param.14), channel_id=1, replica_groups=mesh['groups'=2,'vocab'=4,'edit'=2,'tok'=2] {'vocab'}, dimensions={1}, use_global_device_ids=true | all-gather | bytes 655360 | tf_op jit(solution)/shard_map/all_gather | solution.py:27
  49.7 0.2 multiply_reduce_fusion.3
  49.9 3.9 %fusion.24 = (f32[64]{0:T(128)S(1)}, f32[64,512]{1,0:T(8,128)S(1)}) fusion(bf16[512,4096]{1,0:T(8,128)(2,1)} %param.17, f32[64]{0:T(128)S(1)} %add_rsqrt_fusion.1, f32[4096]{0:T(1024)} %param.16, bf16[64,4096]{1,0:T(8,128)(2,1)S(1)} %all_gather.9), kind=kOutput, calls=%fused_computation.48 | convolution fusion | flops 269516736 | bytes 4866560 | tf_op jit(solution)/shard_map/dot_general | solution.py:33
  53.9 0.4 multiply_reduce_fusion.2
  54.3 0.2 copy-done.2
  54.5 1.6 %fusion.25 = (f32[2,64]{1,0:T(2,128)S(1)}, f32[2,64,512]{2,1,0:T(8,128)S(1)}) fusion(bf16[512,4096]{1,0:T(8,128)(2,1)S(1)} %copy-done.1, f32[4096]{0:T(1024)S(1)} %copy-done.2, f32[2,64]{1,0:T(2,128)S(1)} %get-tuple-element.21, f32[2,4096]{1,0:T(2,128)S(1)} %bitcast.17, f32[64,4096]{1,0:T(8,128)S(1)} %convert_element_type.30, f32[2,64]{1,0:T(2,128)S(1)} %psum.70), kind=kOutput, calls=%fused_computation.49 | convolution fusion | flops 539557760 | bytes 5555712 | tf_op jit(solution)/shard_map/etd,vd->etv/dot_general | solution.py:39
  56.1 18.6 %all-reduce = (f32[64]{0:T(128)S(1)}, f32[2,64]{1,0:T(2,128)S(1)}) all-reduce(f32[64]{0:T(128)S(1)} %get-tuple-element.22, f32[2,64]{1,0:T(2,128)S(1)} %get-tuple-element.24), channel_id=1, replica_groups=mesh['groups'=2,'vocab'=4,'edit'=2,'tok'=2] {'vocab','edit'}, use_global_device_ids=true, to_apply=%region_9.0 | all-reduce | flops 192 | bytes 1536 | tf_op jit(solution)/shard_map/pmax | solution.py:45
  74.7 0.2 fusion.23
  74.9 0.2 multiply_reduce_fusion.4
  75.1 4.9 %all-reduce.2 = (f32[64]{0:T(128)S(1)}, f32[2,64]{1,0:T(2,128)S(1)}, f32[2,64]{1,0:T(2,128)S(1)}, f32[2,64]{1,0:T(2,128)S(1)}) all-reduce(f32[64]{0:T(128)S(1)} %get-tuple-element.18, f32[2,64]{1,0:T(2,128)S(1)} %get-tuple-element.5, ...), channel_id=1, replica_groups=mesh['groups'=2,'vocab'=4,'edit'=2,'tok'=2] {'edit'}, use_global_device_ids=true, to_apply=%region_11.0 | all-reduce | flops 448 | bytes 3584 | tf_op jit(solution)/shard_map/psum | solution.py:52
  80.1 8.3 %all-reduce.1 = (f32[64]{0:T(128)S(1)}, f32[2,64]{1,0:T(2,128)S(1)}, f32[2,64]{1,0:T(2,128)S(1)}, f32[2,64]{1,0:T(2,128)S(1)}) all-reduce(f32[64]{0:T(128)S(1)} %get-tuple-element.12, f32[2,64]{1,0:T(2,128)S(1)} %get-tuple-element.13, ...), channel_id=1, replica_groups=mesh['groups'=2,'vocab'=4,'edit'=2,'tok'=2] {'vocab'}, use_global_device_ids=true, to_apply=%region_12.0 | all-reduce | flops 448 | bytes 3584 | tf_op jit(solution)/shard_map/psum | solution.py:51
  88.4 0.1 subtract_exponential_fusion
  88.5 0.5 constant_dynamic-slice_fusion
  89.1 3.4 %multiply_reduce_fusion.1 = (f32[2,64]{1,0:T(2,128)S(1)}, f32[2,64,4096]{2,1,0:T(8,128)S(1)}) fusion(f32[2,4096]{1,0:T(2,128)S(1)} %bitcast.18, f32[64,4096]{1,0:T(8,128)S(1)} %convert_element_type.30, f32[2,64]{1,0:T(2,128)S(1)} %psum.70, bf16[512,4096]{1,0:T(8,128)(2,1)} %param.17, f32[2,64,512]{2,1,0:T(8,128)S(1)} %get-tuple-element.25, ...), kind=kOutput, calls=%fused_computation.6 | convolution fusion | flops 539754368 | bytes 7784192 | tf_op jit(solution)/shard_map/etv,vd->etd/dot_general | solution.py:62
  92.5 0.8 multiply_reduce_fusion
  93.3 57.6 %psum.75 = f32[2,4096]{1,0:T(2,128)S(1)} all-reduce(f32[2,4096]{1,0:T(2,128)S(1)} %multiply_reduce_fusion), channel_id=1, replica_groups=mesh['groups'=2,'vocab'=4,'edit'=2,'tok'=2] {'vocab','edit','tok'}, use_global_device_ids=true, to_apply=%region_15.0 | all-reduce | flops 8192 | bytes 65536 | tf_op jit(solution)/shard_map/psum | solution.py:69
  150.9 0.7 dynamic_slice.10
  (13 shorter events, 0.2 us)
Async XLA Ops:
  0.6 1.0 copy-start
  49.9 4.4 %copy-start.1 = (bf16[512,4096]{1,0:T(8,128)(2,1)S(1)}, bf16[512,4096]{1,0:T(8,128)(2,1)}, u32[]{:S(2)}) copy-start(bf16[512,4096]{1,0:T(8,128)(2,1)} %param.17) | copy-start | bytes 12582916
  53.8 0.7 copy-start.2
